TPU v7x, 128 devices: a whole 4x4x4 slice. The times are simulated.
128 devices in a mesh: gr: 16 (over y_hi, z, core), gc: 8 (over x, y_lo).
Axes of the slice: x: 4, y: 4 (y_hi: 2, y_lo: 2; y = y_hi * 2 + y_lo), z: 4, core: 2. Of those that a mesh axis runs over, the one named last changes fastest.
Arguments:
- shards: bfloat16 [16, 8, 56, 18432], P('gr', 'gc'), may hold values from -4.5 to 4.5, as said below
- counts: int32 [8, 16], replicated, may hold values from 1 to 56, 448 in all within a row
Outputs:
- next_shards: float32 [16, 8, 56, 18432], P('gr', 'gc')
Inputs may be any that keep to these rules, and one draw needn't show every extreme that they name: Each row of counts sums to 448: the devices (0, c) to (15, c) together hold row block c of the iterate, in order of g. `shards`: rows of a buffer at or beyond its device's count are not part of the iterate and hold arbitrary values.
All inputs are finite; a program needn't handle non-finite values.
Results may differ from a plain program's by a relative error of at most 0.0003.
Values may be sent and summed in bfloat16 or wider, within the bound.
A program may use at most 128 MiB of HBM per device.

v0:
```python
import jax
import jax.numpy as jnp
from jax import lax
from jax.sharding import PartitionSpec as P

M = 3584
N = 18432
linear_coef = 3.4445
cubic_coef = -4.775
quintic_coef = 2.0315
highest = lax.Precision.HIGHEST


def rows_against(left_rows, right_rows):
    return lax.dot_general(
        left_rows, right_rows, (((1,), (1,)), ((), ())), preferred_element_type=jnp.float32
    )


def make_accumulate(panel, sub_width, running, segment):
    seg_width = segment.shape[1]

    def one_turn(turn_index, summed):
        seg_part = lax.dynamic_slice_in_dim(segment, turn_index * sub_width, sub_width, 1)
        panel_rows = lax.dynamic_slice_in_dim(panel, turn_index * sub_width, sub_width, 0).astype(
            jnp.float32
        )
        return summed + jnp.dot(
            seg_part, panel_rows, precision=highest, preferred_element_type=jnp.float32
        )

    return lax.fori_loop(0, seg_width // sub_width, one_turn, running)


def body(shards, counts):
    own_rows = shards[0, 0]
    grid_rows = lax.axis_size("gr")
    grid_cols = lax.axis_size("gc")
    row_block = lax.axis_index("gc")
    capacity = own_rows.shape[0]
    full_width = own_rows.shape[1]
    col_width = full_width // grid_rows
    block_rows = M // grid_cols
    gram_width = M // grid_rows
    my_counts = lax.dynamic_index_in_dim(counts, row_block, 0, keepdims=False)
    my_starts = jnp.cumsum(my_counts) - my_counts
    received = lax.all_to_all(own_rows, "gr", split_axis=1, concat_axis=0, tiled=True)
    position = jnp.arange(block_rows, dtype=jnp.int32)
    holder = jnp.sum((my_starts[None, :] <= position[:, None]).astype(jnp.int32), axis=1) - 1
    one_hot = holder[:, None] == jnp.arange(grid_rows, dtype=jnp.int32)[None, :]
    first_row = jnp.sum(jnp.where(one_hot, my_starts[None, :], 0), axis=1)
    source_rows = holder * capacity + position - first_row
    own_block = jnp.take(received, source_rows, axis=0)
    panel = lax.all_gather(own_block, "gc", axis=0, tiled=True)
    partial_value = rows_against(own_block, panel)
    gram_block = lax.psum_scatter(partial_value, "gr", scatter_dimension=1, tiled=True) / N
    gram_cols = lax.all_gather(gram_block, "gc", axis=0, tiled=True)
    square_part = lax.dot_general(
        gram_block,
        gram_cols,
        (((1,), (1,)), ((), ())),
        precision=highest,
        preferred_element_type=jnp.float32,
    )
    square_block = lax.psum_scatter(square_part, "gr", scatter_dimension=1, tiled=True)
    poly_block = cubic_coef * gram_block + quintic_coef * square_block
    start_sum = jnp.zeros((block_rows, col_width), jnp.float32)
    product = make_accumulate(
        panel, gram_width, start_sum, lax.all_gather(poly_block, "gr", axis=1, tiled=True)
    )
    update_block = linear_coef * own_block.astype(jnp.float32) + product
    slot_ids = jnp.arange(capacity, dtype=jnp.int32)
    target_rows = jnp.minimum(my_starts[:, None] + slot_ids[None, :], block_rows - 1).reshape(-1)
    is_live = (slot_ids[None, :] < my_counts[:, None]).reshape(-1)
    outgoing = jnp.where(
        is_live[:, None], jnp.take(update_block, target_rows, axis=0), jnp.zeros((), jnp.float32)
    )
    returned = lax.all_to_all(outgoing, "gr", split_axis=0, concat_axis=1, tiled=True)
    return returned.reshape(1, 1, capacity, full_width)


def solution(mesh):
    placed = (P("gr", "gc", None, None), P())
    return jax.shard_map(
        body, mesh=mesh, in_specs=placed, out_specs=P("gr", "gc", None, None), check_vma=False
    )
```

profile of v0, /device:TPU:1, one launch (start us, length us, event | category | flops | bytes accessed | tf_op | source)
XLA Modules:
  0.0 709.8 jit_solution(17190910258514315236)
XLA Ops:
  6.5 1.8 copy.24
  8.4 0.0 copy-start.1
  8.4 1.7 copy.15
  10.1 9.5 %all-to-all-start = ((bf16[56,16,1152]{2,0,1:T(8,128)(2,1)}), bf16[56,16,1152]{2,0,1:T(8,128)(2,1)S(1)}, u32[]{:S(2)}, u32[]{:S(2)}) async-start(bf16[56,16,1152]{2,0,1:T(8,128)(2,1)} %copy.15), calls=%async_computation | async-start | bytes 4128768 | tf_op jit(solution)/shard_map/all_to_all | solution.py:47
  19.5 0.0 all-gather.4.cloned.1.call-start
  19.6 0.0 copy-done.1
  19.6 0.1 copy.14
  19.7 0.1 reduce
  19.8 0.1 convert_reduce_fusion
  19.9 0.1 select_reduce_fusion
  20.1 27.6 %all-to-all-done = bf16[56,16,1152]{2,0,1:T(8,128)(2,1)S(1)} async-done(((bf16[56,16,1152]{2,0,1:T(8,128)(2,1)}), bf16[56,16,1152]{2,0,1:T(8,128)(2,1)S(1)}, u32[]{:S(2)}, u32[]{:S(2)}) %all-to-all-start) | async-done | bytes 2064416 | tf_op jit(solution)/shard_map/all_to_all | solution.py:47
  47.6 2.3 gather_fusion
  49.9 1.1 broadcast_select_fusion
  51.1 0.0 all-gather.4.cloned.1.call-update
  51.1 0.0 reduce-scatter.7.cloned.1.call-start
  51.2 166.8 %all-gather.4.cloned.1.call-done = bf16[3584,1152]{1,0:T(8,128)(2,1)} async-done(((bf16[448,1152]{1,0:T(8,128)(2,1)}), bf16[3584,1152]{1,0:T(8,128)(2,1)}) %all-gather.4.cloned.1.call-update) | async-done | bytes 8257552 | tf_op jit(solution)/shard_map/all_gather | solution.py:54
  218.0 11.7 %convolution_bitcast_fusion.1 = f32[3584,448]{1,0:T(8,128)} fusion(bf16[448,1152]{1,0:T(8,128)(2,1)} %broadcast_select_fusion, bf16[3584,1152]{1,0:T(8,128)(2,1)} %all-gather.4.cloned.1.call-done), kind=kOutput, calls=%fused_computation.7 | convolution fusion | flops 3699376128 | bytes 15712256
  229.7 0.0 reduce-scatter.7.cloned.1.call-update
  229.7 0.0 all-gather.6.cloned.1.call-start
  229.7 98.5 %reduce-scatter.7.cloned.1.call-done = f32[224,448]{1,0:T(8,128)} async-done(((f32[3584,448]{1,0:T(8,128)}), f32[224,448]{1,0:T(8,128)}) %reduce-scatter.7.cloned.1.call-update) | async-done | bytes 401424
  328.2 1.2 copy.20
  329.4 0.8 broadcast_multiply_fusion
  330.3 0.0 all-gather.6.cloned.1.call-update
  330.3 0.0 reduce-scatter.9.cloned.1.call-start
  330.3 80.0 %all-gather.6.cloned.1.call-done = f32[3584,224]{1,0:T(8,128)} async-done(((f32[448,224]{1,0:T(8,128)}), f32[3584,224]{1,0:T(8,128)}) %all-gather.6.cloned.1.call-update) | async-done | bytes 3211280 | tf_op jit(solution)/shard_map/all_gather | solution.py:57
  410.3 10.0 %convolution_bitcast_fusion = f32[3584,448]{1,0:T(8,128)} fusion(f32[3584,224]{1,0:T(8,128)} %all-gather.6.cloned.1.call-done, f32[448,224]{1,0:T(8,128)S(1)} %copy.20), kind=kOutput, calls=%fused_computation.6 | convolution fusion | flops 4316039168 | bytes 10035200
  420.3 0.0 reduce-scatter.9.cloned.1.call-update
  420.4 0.2 all-gather.8.cloned.1.call-start
  420.6 94.1 %reduce-scatter.9.cloned.1.call-done = f32[224,448]{1,0:T(8,128)} async-done(((f32[3584,448]{1,0:T(8,128)}), f32[224,448]{1,0:T(8,128)}) %reduce-scatter.9.cloned.1.call-update) | async-done | bytes 401424
  514.7 1.2 copy.22
  515.9 0.1 multiply_add_fusion.1
  516.0 1.0 copy.16
  516.9 0.0 all-gather.8.cloned.1.call-update
  517.0 0.1 add_minimum_fusion
  517.0 0.1 min.22
  517.2 0.1 iota_compare_fusion.2
  517.3 69.1 %all-gather.8.cloned.1.call-done = f32[448,3584]{0,1:T(8,128)} async-done(((f32[448,224]{0,1:T(8,128)}), f32[448,3584]{0,1:T(8,128)}) %all-gather.8.cloned.1.call-update) | async-done | bytes 6422544 | tf_op jit(solution)/shard_map/all_gather | solution.py:69
  586.3 46.5 %while.14 = (s32[]{:T(128)}, f32[448,1152]{1,0:T(8,128)S(1)}, f32[448,3584]{0,1:T(8,128)}, bf16[3584,1152]{1,0:T(8,128)(2,1)}, s32[]{:T(128)}, /*index=5*/s32[]{:T(128)}, s32[]{:T(128)}, s32[]{:T(128)}) while((s32[]{:T(128)}, f32[448,1152]{1,0:T(8,128)S(1)}, f32[448,3584]{0,1:T(8,128)}, bf16[3584,1152]{1,0:T(8,128)(2,1)}, ...), condition=%wide.region_6.7_spmd.clone, body=%wide.region_5.6_spmd.clone.sunk | while | flops 1388298240 | bytes 5105292 | solution.py:32
  586.3 2.9 convolution_add_fusion.2
  589.2 2.9 convolution_add_fusion.2
  592.1 2.9 convolution_add_fusion.2
  595.0 2.9 convolution_add_fusion.2
  597.9 2.9 convolution_add_fusion.2
  600.9 2.9 convolution_add_fusion.2
  603.8 2.9 convolution_add_fusion.2
  606.7 2.9 convolution_add_fusion.2
  609.6 2.9 convolution_add_fusion.2
  612.5 2.9 convolution_add_fusion.2
  615.4 2.9 convolution_add_fusion.2
  618.3 2.9 convolution_add_fusion.2
  621.2 2.9 convolution_add_fusion.2
  624.1 2.9 convolution_add_fusion.2
  627.0 2.9 convolution_add_fusion.2
  629.9 2.9 convolution_add_fusion.2
  632.8 0.0 copy-start
  632.8 1.3 copy-done
  634.1 1.9 multiply_add_fusion
  636.0 4.3 gather_fusion.1
  640.4 2.5 select_select_fusion
  642.9 52.7 %all_to_all.32 = f32[16,56,1152]{2,1,0:T(8,128)S(1)} all-to-all(f32[16,56,1152]{2,1,0:T(8,128)S(1)} %select_select_fusion), channel_id=1, replica_groups=mesh['gr'=16,'gc'=8] {'gr'}, dimensions={0} | all-to-all | bytes 8257536 | tf_op jit(solution)/shard_map/all_to_all | solution.py:78
  695.6 2.7 copy.18
  698.3 5.0 reshape.143
  (12 shorter events, 0.1 us)
Async XLA Ops:
  8.4 11.2 %copy-start.1 = (s32[8,16]{1,0:T(8,128)S(1)}, s32[8,16]{1,0:T(8,128)}, u32[]{:S(2)}) copy-start(s32[8,16]{1,0:T(8,128)} %param.5) | copy-start | bytes 1540
  10.1 37.6 %all-to-all-start = ((bf16[56,16,1152]{2,0,1:T(8,128)(2,1)}), bf16[56,16,1152]{2,0,1:T(8,128)(2,1)S(1)}, u32[]{:S(2)}, u32[]{:S(2)}) async-start(bf16[56,16,1152]{2,0,1:T(8,128)(2,1)} %copy.15), calls=%async_computation | async-start | bytes 4128768 | tf_op jit(solution)/shard_map/all_to_all | solution.py:47
  19.5 198.5 %all-gather.4.cloned.1.call-start = ((), (), s32[]{:S(2)}) async-start(), calls=%async_computation.4 | async-start | bytes 9289728 | tf_op jit(solution)/shard_map/all_gather | solution.py:54
  51.1 277.1 %reduce-scatter.7.cloned.1.call-start = ((), (), s32[]{:S(2)}) async-start(), calls=%async_computation.7 | async-start | bytes 7798784
  229.7 180.6 %all-gather.6.cloned.1.call-start = ((), (), s32[]{:S(2)}) async-start(), calls=%async_computation.5 | async-start | bytes 4128768 | tf_op jit(solution)/shard_map/all_gather | solution.py:57
  330.3 184.4 %reduce-scatter.9.cloned.1.call-start = ((), (), s32[]{:S(2)}) async-start(), calls=%async_computation.8 | async-start | bytes 7798784
  420.4 166.0 %all-gather.8.cloned.1.call-start = ((), (), s32[]{:S(2)}) async-start(), calls=%async_computation.6 | async-start | bytes 7798784 | tf_op jit(solution)/shard_map/all_gather | solution.py:69
  632.8 1.3 copy-start
Sparse Core Ops, SparseCore 0:
  51.2 166.7 all-gather.3
  229.8 98.3 reduce-scatter.6
  330.4 79.8 all-gather.5
  420.5 94.1 reduce-scatter.8
  517.1 69.2 all-gather.7
where the time goes:
time: 711 us; the launch traced here: 710 us
  waiting for transfers between devices  536 us (75%)
  matrix products  67.7 us (10%)
  blocking collectives  52.7 us (7%)
  local copies, waits for them, and re-layouts  22.7 us (3%)
  between operations  13.3 us (2%)
  starting transfers between devices  9.85 us (1%)
    unnamed x7, waiting for transfers between devices  193 us
    all_gather x1, waiting for transfers between devices, body(): panel = lax.all_gather(own_block, 'gc', axis=0, tiled=True)  167 us
    all_gather x1, waiting for transfers between devices, body(): gram_cols = lax.all_gather(gram_block, 'gc', axis=0, tiled=True)  80 us
    all_gather x1, waiting for transfers between devices, body(): lax.all_gather(poly_block, 'gr', axis=1, tiled=True)  69.1 us
    all_to_all x1, blocking collectives, body(): lax.all_to_all(outgoing, 'gr', split_axis=0, concat_axis=1, tiled=True)  52.7 us
    dot_general x16, matrix products, one_turn(): jnp.dot(seg_part, panel_rows, precision=highest, preferred_element_type=j...  46 us
    all_to_all x1, waiting for transfers between devices, body(): lax.all_to_all(own_rows, 'gr', split_axis=1, concat_axis=0, tiled=True)  27.6 us
    unnamed x2, matrix products  21.7 us
  transfers between devices with their start and end apart: 6, of which 6 were waited for; matrix products, arithmetic and copies ran while one was open for 0% of the time, Pallas kernels for 0%

commit v1 on v0

--- a/solution.py
+++ b/solution.py
@@ -51,7 +51,9 @@
     first_row = jnp.sum(jnp.where(one_hot, my_starts[None, :], 0), axis=1)
     source_rows = holder * capacity + position - first_row
     own_block = jnp.take(received, source_rows, axis=0)
-    panel = lax.all_gather(own_block, "gc", axis=0, tiled=True)
+    panel = jnp.concatenate(
+        lax.all_to_all(jnp.stack([own_block] * lax.axis_size("gc")), "gc", 0, 0), axis=0
+    )
     partial_value = rows_against(own_block, panel)
     gram_block = lax.psum_scatter(partial_value, "gr", scatter_dimension=1, tiled=True) / N
     gram_cols = lax.all_gather(gram_block, "gc", axis=0, tiled=True)

time: 711 us -> 634 us (0.89)
  waiting for transfers between devices: 536 us -> 365 us
  blocking collectives: 52.7 us -> 148 us
    all_gather x1 -> x0, waiting for transfers between devices: 167 us -> none  [body(): panel = lax.all_gather(own_block, 'gc', axis=0, tiled=True)]
    all_to_all x0 -> x1, blocking collectives: none -> 95.6 us  [body(): lax.all_to_all(jnp.stack([own_block] * lax.axis_size('gc')), 'gc', 0, 0)]
    unnamed x7 -> x6, waiting for transfers between devices: 193 us -> 188 us
  transfers between devices with their start and end apart: 6 -> 5, of which waited for: 6 -> 5; matrix products, arithmetic and copies ran while one was open for 0% -> 0% of each run, Pallas kernels for 0% -> 0%
where the time goes in v1:
time: 634 us; the launch traced here: 633 us
  waiting for transfers between devices  365 us (58%)
  blocking collectives  148 us (23%)
  matrix products  63.1 us (10%)
  local copies, waits for them, and re-layouts  26.9 us (4%)
  between operations  13.3 us (2%)
  starting transfers between devices  9.8 us (2%)
    unnamed x6, waiting for transfers between devices  188 us
    all_to_all x1, blocking collectives, body(): lax.all_to_all(jnp.stack([own_block] * lax.axis_size('gc')), 'gc', 0, 0)  95.6 us
    all_gather x1, waiting for transfers between devices, body(): gram_cols = lax.all_gather(gram_block, 'gc', axis=0, tiled=True)  80.1 us
    all_gather x1, waiting for transfers between devices, body(): lax.all_gather(poly_block, 'gr', axis=1, tiled=True)  69.1 us
    all_to_all x1, blocking collectives, body(): lax.all_to_all(outgoing, 'gr', split_axis=0, concat_axis=1, tiled=True)  52.7 us
    dot_general x16, matrix products, one_turn(): jnp.dot(seg_part, panel_rows, precision=highest, preferred_element_type=j...  46 us
    all_to_all x1, waiting for transfers between devices, body(): lax.all_to_all(own_rows, 'gr', split_axis=1, concat_axis=0, tiled=True)  27.6 us
    unnamed x2, matrix products  17.1 us
  transfers between devices with their start and end apart: 5, of which 5 were waited for; matrix products, arithmetic and copies ran while one was open for 0% of the time, Pallas kernels for 0%

profile of v1, /device:TPU:1, one launch (start us, length us, event | category | flops | bytes accessed | tf_op | source)
XLA Modules:
  0.0 633.2 jit_solution(17714890843271205389)
XLA Ops:
  6.5 1.8 copy.24
  8.4 0.0 copy-start.2
  8.4 1.7 copy.15
  10.1 9.5 %all-to-all-start = ((bf16[56,16,1152]{2,0,1:T(8,128)(2,1)}), bf16[56,16,1152]{2,0,1:T(8,128)(2,1)S(1)}, u32[]{:S(2)}, u32[]{:S(2)}) async-start(bf16[56,16,1152]{2,0,1:T(8,128)(2,1)} %copy.15), calls=%async_computation | async-start | bytes 4128768 | tf_op jit(solution)/shard_map/all_to_all | solution.py:47
  19.5 0.0 reduce-scatter.7.cloned.1.call-start
  19.6 0.0 copy-done.2
  19.6 0.1 copy.14
  19.7 0.1 reduce
  19.8 0.1 convert_reduce_fusion
  19.9 0.1 select_reduce_fusion
  20.1 27.6 %all-to-all-done = bf16[56,16,1152]{2,0,1:T(8,128)(2,1)S(1)} async-done(((bf16[56,16,1152]{2,0,1:T(8,128)(2,1)}), bf16[56,16,1152]{2,0,1:T(8,128)(2,1)S(1)}, u32[]{:S(2)}, u32[]{:S(2)}) %all-to-all-start) | async-done | bytes 2064416 | tf_op jit(solution)/shard_map/all_to_all | solution.py:47
  47.6 2.3 gather_fusion
  49.9 0.2 broadcast_select_fusion
  50.1 1.1 stack.2
  51.2 95.6 %all_to_all.37 = bf16[8,448,1152]{2,1,0:T(8,128)(2,1)S(1)} all-to-all(bf16[8,448,1152]{2,1,0:T(8,128)(2,1)S(1)} %stack.2), channel_id=1, replica_groups=mesh['gr'=16,'gc'=8] {'gc'}, dimensions={0} | all-to-all | bytes 16515072 | tf_op jit(solution)/shard_map/all_to_all | solution.py:55
  146.8 0.0 copy-start.1
  146.8 3.2 copy-done.1
  150.0 7.1 %convolution_bitcast_fusion.1 = f32[3584,448]{1,0:T(8,128)} fusion(bf16[448,1152]{1,0:T(8,128)(2,1)S(1)} %broadcast_select_fusion, bf16[3584,1152]{1,0:T(8,128)(2,1)S(1)} %bitcast.36), kind=kOutput, calls=%fused_computation.7 | convolution fusion | flops 3699376128 | bytes 15712256
  157.1 0.0 reduce-scatter.7.cloned.1.call-update
  157.2 0.0 all-gather.3.cloned.1.call-start
  157.2 94.3 %reduce-scatter.7.cloned.1.call-done = f32[224,448]{1,0:T(8,128)} async-done(((f32[3584,448]{1,0:T(8,128)}), f32[224,448]{1,0:T(8,128)}) %reduce-scatter.7.cloned.1.call-update) | async-done | bytes 401424
  251.5 1.2 copy.20
  252.7 0.8 broadcast_multiply_fusion
  253.6 0.0 all-gather.3.cloned.1.call-update
  253.6 0.0 reduce-scatter.9.cloned.1.call-start
  253.6 80.1 %all-gather.3.cloned.1.call-done = f32[3584,224]{1,0:T(8,128)} async-done(((f32[448,224]{1,0:T(8,128)}), f32[3584,224]{1,0:T(8,128)}) %all-gather.3.cloned.1.call-update) | async-done | bytes 3211280 | tf_op jit(solution)/shard_map/all_gather | solution.py:59
  333.7 10.0 %convolution_bitcast_fusion = f32[3584,448]{1,0:T(8,128)} fusion(f32[3584,224]{1,0:T(8,128)} %all-gather.3.cloned.1.call-done, f32[448,224]{1,0:T(8,128)S(1)} %copy.20), kind=kOutput, calls=%fused_computation.6 | convolution fusion | flops 4316039168 | bytes 10035200
  343.7 0.0 reduce-scatter.9.cloned.1.call-update
  343.7 0.2 all-gather.5.cloned.1.call-start
  343.9 94.1 %reduce-scatter.9.cloned.1.call-done = f32[224,448]{1,0:T(8,128)} async-done(((f32[3584,448]{1,0:T(8,128)}), f32[224,448]{1,0:T(8,128)}) %reduce-scatter.9.cloned.1.call-update) | async-done | bytes 401424
  438.0 1.2 copy.22
  439.2 0.1 multiply_add_fusion.1
  439.3 1.0 copy.16
  440.3 0.0 all-gather.5.cloned.1.call-update
  440.3 0.1 add_minimum_fusion
  440.4 0.1 min.22
  440.6 0.1 iota_compare_fusion.2
  440.6 69.1 %all-gather.5.cloned.1.call-done = f32[448,3584]{0,1:T(8,128)} async-done(((f32[448,224]{0,1:T(8,128)}), f32[448,3584]{0,1:T(8,128)}) %all-gather.5.cloned.1.call-update) | async-done | bytes 6422544 | tf_op jit(solution)/shard_map/all_gather | solution.py:71
  509.7 46.5 %while.14 = (s32[]{:T(128)}, f32[448,1152]{1,0:T(8,128)S(1)}, f32[448,3584]{0,1:T(8,128)}, bf16[3584,1152]{1,0:T(8,128)(2,1)}, s32[]{:T(128)}, /*index=5*/s32[]{:T(128)}, s32[]{:T(128)}, s32[]{:T(128)}) while((s32[]{:T(128)}, f32[448,1152]{1,0:T(8,128)S(1)}, f32[448,3584]{0,1:T(8,128)}, bf16[3584,1152]{1,0:T(8,128)(2,1)}, ...), condition=%wide.region_6.7_spmd.clone, body=%wide.region_5.6_spmd.clone.sunk | while | flops 1388298240 | bytes 5105292 | solution.py:32
  509.7 2.9 convolution_add_fusion.2
  512.6 2.9 convolution_add_fusion.2
  515.5 2.9 convolution_add_fusion.2
  518.4 2.9 convolution_add_fusion.2
  521.3 2.9 convolution_add_fusion.2
  524.2 2.9 convolution_add_fusion.2
  527.1 2.9 convolution_add_fusion.2
  530.0 2.9 convolution_add_fusion.2
  532.9 2.9 convolution_add_fusion.2
  535.8 2.9 convolution_add_fusion.2
  538.8 2.9 convolution_add_fusion.2
  541.7 2.9 convolution_add_fusion.2
  544.6 2.9 convolution_add_fusion.2
  547.5 2.9 convolution_add_fusion.2
  550.4 2.9 convolution_add_fusion.2
  553.3 2.9 convolution_add_fusion.2
  556.2 0.0 copy-start
  556.2 1.3 copy-done
  557.5 1.9 multiply_add_fusion
  559.4 4.3 gather_fusion.1
  563.7 2.5 select_select_fusion
  566.2 52.7 %all_to_all.38 = f32[16,56,1152]{2,1,0:T(8,128)S(1)} all-to-all(f32[16,56,1152]{2,1,0:T(8,128)S(1)} %select_select_fusion), channel_id=1, replica_groups=mesh['gr'=16,'gc'=8] {'gr'}, dimensions={0} | all-to-all | bytes 8257536 | tf_op jit(solution)/shard_map/all_to_all | solution.py:80
  619.0 2.7 copy.18
  621.6 5.0 reshape.154
  (12 shorter events, 0.1 us)
Async XLA Ops:
  8.4 11.2 %copy-start.2 = (s32[8,16]{1,0:T(8,128)S(1)}, s32[8,16]{1,0:T(8,128)}, u32[]{:S(2)}) copy-start(s32[8,16]{1,0:T(8,128)} %param.5) | copy-start | bytes 1540
  10.1 37.6 %all-to-all-start = ((bf16[56,16,1152]{2,0,1:T(8,128)(2,1)}), bf16[56,16,1152]{2,0,1:T(8,128)(2,1)S(1)}, u32[]{:S(2)}, u32[]{:S(2)}) async-start(bf16[56,16,1152]{2,0,1:T(8,128)(2,1)} %copy.15), calls=%async_computation | async-start | bytes 4128768 | tf_op jit(solution)/shard_map/all_to_all | solution.py:47
  19.5 232.0 %reduce-scatter.7.cloned.1.call-start = ((), (), s32[]{:S(2)}) async-start(), calls=%async_computation.7 | async-start | bytes 7798784
  146.8 3.2 copy-start.1
  157.2 176.5 %all-gather.3.cloned.1.call-start = ((), (), s32[]{:S(2)}) async-start(), calls=%async_computation.5 | async-start | bytes 4128768 | tf_op jit(solution)/shard_map/all_gather | solution.py:59
  253.6 184.5 %reduce-scatter.9.cloned.1.call-start = ((), (), s32[]{:S(2)}) async-start(), calls=%async_computation.8 | async-start | bytes 7798784
  343.7 166.0 %all-gather.5.cloned.1.call-start = ((), (), s32[]{:S(2)}) async-start(), calls=%async_computation.6 | async-start | bytes 7798784 | tf_op jit(solution)/shard_map/all_gather | solution.py:71
  556.2 1.3 copy-start
Sparse Core Ops, SparseCore 0:
  157.3 94.2 reduce-scatter.6
  253.7 79.9 all-gather.2
  343.8 94.1 reduce-scatter.8
  440.4 69.2 all-gather.4
